TPU v7x, 32 devices: a whole 2x2x4 slice. The times are simulated.
32 devices in a mesh: row: 8 (over y, x, core), col: 4 (over z).
Axes of the slice: x: 2, y: 2, z: 4, core: 2. Of those that a mesh axis runs over, the one named last changes fastest.
Arguments:
- tiles: bfloat16 [8, 64, 128, 128], P('row', 'col'), may hold values from -2 to 2
- tile_index: int32 [8, 64], P('row', 'col'), may hold values from 0 to 16384, as said below
- u_basis: float32 [64, 131072], P(None, ('row', 'col')), may hold values from -10 to 10
- v_basis: float32 [64, 4, 16384], P(None, 'col', 'row'), may hold values from -10 to 10
- v_start: float32 [65536], P('col'), may hold values from -0.5 to 1.5
Outputs:
- left_vectors: float32 [2, 131072], P(None, ('row', 'col'))
- right_vectors: float32 [2, 4, 16384], P(None, 'col', 'row')
- bidiagonal: float32 [2, 2], replicated
Inputs may be any that keep to these rules, and one draw needn't show every extreme that they name: `tile_index`: each block's 16 slots name distinct tiles of its 128 x 128 block as r * 128 + c; the value 128 * 128 marks an empty slot, and empty slots come after all live ones. Blocks have different numbers of live slots, at least 4; some block has all 16 slots live.
All inputs are finite; a program needn't handle non-finite values.
Results may differ from a plain program's by a relative error of at most 0.0003.
Values sent between devices are 32-bit elements; how exact they have to be, the bound alone decides.
No kernel may reach another device: no remote copies, remote signals or barrier semaphores. Data moves between devices by JAX's collectives and lax.ppermute only.
A program may use at most 64 MiB of HBM per device.

v0:
```python
import jax
import jax.numpy as jnp
from jax import lax
from jax.sharding import PartitionSpec as P

ITERS = 2
HIGHEST = lax.Precision.HIGHEST
EPSILON = 1e-06


def project_gram(share, basis, gram, total):
    coeffs, squares = lax.psum(
        (jnp.dot(basis, share, precision=HIGHEST), jnp.sum(share * share)), ("row", "col")
    )
    coeffs = coeffs / total
    squares = squares / total
    second = coeffs - jnp.dot(gram, coeffs, precision=HIGHEST)
    combined = coeffs + second
    gram_comb = jnp.dot(gram, combined, precision=HIGHEST)
    remaining = coeffs - gram_comb
    squared = (
        squares
        - 2.0 * jnp.dot(combined, coeffs, precision=HIGHEST)
        + jnp.dot(combined, gram_comb, precision=HIGHEST)
    )
    scale = jnp.sqrt(squared + EPSILON)
    unit = (share - jnp.dot(combined, basis, precision=HIGHEST)) / scale
    column = remaining / scale
    corner = squared / (scale * scale)
    upper = jnp.concatenate([gram, column[:, None]], 1)
    lower = jnp.concatenate([column, corner[None]])[None, :]
    return (unit, scale, jnp.concatenate([upper, lower], 0), combined)


def shards(tiles, tile_index, u_basis, v_basis, v_start):
    blocks = tiles[0].astype(jnp.float32)
    slots = tile_index[0]
    width = blocks.shape[1]
    cols_len = v_start.shape[0]
    col_blocks = cols_len // width
    row_count = lax.axis_size("row")
    col_count = lax.axis_size("col")
    left_piece = u_basis.shape[1]
    right_piece = v_basis.shape[2]
    rows_len = left_piece * col_count
    row_blocks = rows_len // width
    total_left = rows_len * row_count
    total_right = cols_len * col_count
    rows_hot = (slots[:, None] // col_blocks == jnp.arange(row_blocks)[None, :]).astype(jnp.float32)
    cols_hot = (slots[:, None] % col_blocks == jnp.arange(col_blocks)[None, :]).astype(jnp.float32)
    left_start = lax.axis_index("col") * left_piece
    right_start = lax.axis_index("row") * right_piece

    def forward_many(vectors):
        count = vectors.shape[0]
        picked = jnp.einsum(
            "tc,mck->mtk", cols_hot, vectors.reshape(count, col_blocks, width), precision=HIGHEST
        )
        product = jnp.einsum("tab,mtb->mta", blocks, picked, precision=HIGHEST)
        return jnp.einsum("tr,mta->mra", rows_hot, product, precision=HIGHEST).reshape(
            count, rows_len
        )

    def forward(vector):
        return forward_many(vector[None, :])[0]

    left_basis = u_basis
    start_share = lax.dynamic_slice_in_dim(v_start, right_start, right_piece)
    right_basis = jnp.concatenate([v_basis[:, 0, :], start_share[None, :]], 0)
    left_gram, right_gram = lax.psum(
        (
            jnp.dot(left_basis, left_basis.T, precision=HIGHEST),
            jnp.dot(right_basis, right_basis.T, precision=HIGHEST),
        ),
        ("row", "col"),
    )
    left_gram = left_gram / total_left
    right_gram = right_gram / total_right
    forward_now = forward(v_start)
    lefts, rights, alphas, betas = ([], [], [], [])
    for iteration in range(ITERS):
        left_whole = lax.psum(forward_now, "col")
        left_result = lax.dynamic_slice_in_dim(left_whole, left_start, left_piece)
        share = left_result
        left_unit, alpha, left_gram, combined = project_gram(
            share, left_basis, left_gram, total_left
        )
        left_basis = jnp.concatenate([left_basis, left_unit[None, :]], 0)
        join_joined = lax.all_gather(left_unit, "col", axis=0, tiled=True)
        backward_vectors = join_joined[None, :]
        backward_count = backward_vectors.shape[0]
        backward_picked = jnp.einsum(
            "tr,mrk->mtk",
            rows_hot,
            backward_vectors.reshape(backward_count, row_blocks, width),
            precision=HIGHEST,
        )
        backward_product = jnp.einsum("tab,mta->mtb", blocks, backward_picked, precision=HIGHEST)
        backward_now = jnp.einsum(
            "tc,mtb->mcb", cols_hot, backward_product, precision=HIGHEST
        ).reshape(backward_count, cols_len)[0]
        whole = lax.psum(backward_now, "row")
        result = lax.dynamic_slice_in_dim(whole, right_start, right_piece)
        share = result
        right_unit, beta, right_gram, combined = project_gram(
            share, right_basis, right_gram, total_right
        )
        right_basis = jnp.concatenate([right_basis, right_unit[None, :]], 0)
        if iteration + 1 < ITERS:
            joined = lax.all_gather(right_unit, "row", axis=0, tiled=True)
            forward_now = forward(joined)
        lefts.append(left_unit)
        rights.append(right_unit)
        alphas.append(alpha)
        betas.append(beta)
    left_vectors = jnp.stack(lefts)
    right_vectors = jnp.stack(rights)[:, None, :]
    bidiagonal = jnp.stack([jnp.stack(alphas), jnp.stack(betas)])
    return (left_vectors, right_vectors, bidiagonal)


def solution(mesh):
    placed = (
        P("row", "col", None, None),
        P("row", "col"),
        P(None, ("row", "col")),
        P(None, "col", "row"),
        P("col"),
    )
    return jax.shard_map(
        shards,
        mesh=mesh,
        in_specs=placed,
        out_specs=(P(None, ("row", "col")), P(None, "col", "row"), P()),
        check_vma=False,
    )
```

profile of v0, /device:TPU:0, one launch (start us, length us, event | category | flops | bytes accessed | tf_op | source)
XLA Modules:
  0.0 422.3 jit_solution(5851223043497568862)
XLA Ops:
  7.9 1.0 fusion.30
  9.0 0.9 fusion.19
  11.0 2.8 fusion.72
  15.4 32.7 %all-reduce.9.cloned.1.call-done = f32[16384]{0:T(1024)} async-done(((f32[16384]{0:T(1024)}), f32[16384]{0:T(1024)}) %all-reduce.9.cloned.1.call-update) | async-done | bytes 65552 | tf_op jit(solution)/shard_map/psum | solution.py:82
  48.1 1.3 multiply_reduce_fusion.1
  49.4 0.9 convolution_bitcast_fusion.5
  50.3 40.5 %all-reduce.3 = (f32[64]{0:T(128)S(1)}, f32[64,64]{1,0:T(8,128)S(1)}, f32[]{:T(128)}) all-reduce(f32[64]{0:T(128)S(1)} %convolution_bitcast_fusion.5, f32[64,64]{1,0:T(8,128)S(1)} %fusion.72, f32[]{:T(128)} %get-tuple-element.23), channel_id=1, replica_groups=mesh['row'=8,'col'=4] {'row','col'}, use_global_device_ids=true, to_apply=%region_1.2 | all-reduce | flops 4161 | bytes 33288 | tf_op jit(solution)/shard_map/psum | solution.py:12
  94.4 13.3 %all_gather.9 = f32[16384]{0:T(1024)S(1)} all-gather(f32[4096]{0:T(1024)S(1)} %subtract_divide_fusion.1), channel_id=1, replica_groups=mesh['row'=8,'col'=4] {'col'}, dimensions={0}, use_global_device_ids=true | all-gather | bytes 81920 | tf_op jit(solution)/shard_map/all_gather | solution.py:89
  109.7 52.5 %all-reduce.11.cloned.1.call-done = f32[16384]{0:T(1024)} async-done(((f32[16384]{0:T(1024)}), f32[16384]{0:T(1024)}) %all-reduce.11.cloned.1.call-update) | async-done | bytes 65552 | tf_op jit(solution)/shard_map/psum | solution.py:102
  162.2 1.3 multiply_reduce_fusion.3
  164.1 39.8 %all-reduce.2 = (f32[65]{0:T(128)S(1)}, f32[65,65]{1,0:T(8,128)S(1)}, f32[]{:T(128)}) all-reduce(f32[65]{0:T(128)S(1)} %convolution_bitcast_fusion.15, f32[65,65]{1,0:T(8,128)S(1)} %fusion.23, f32[]{:T(128)} %get-tuple-element.21), channel_id=1, replica_groups=mesh['row'=8,'col'=4] {'row','col'}, use_global_device_ids=true, to_apply=%region_6.7 | all-reduce | flops 4291 | bytes 34328 | tf_op jit(solution)/shard_map/psum | solution.py:12
  204.5 0.9 multiply_reduce_fusion.6
  207.4 10.0 %all_gather.10 = f32[16384]{0:T(1024)S(1)} all-gather(f32[2048]{0:T(1024)S(1)} %subtract_divide_fusion.3), channel_id=1, replica_groups=mesh['row'=8,'col'=4] {'row'}, dimensions={0}, use_global_device_ids=true | all-gather | bytes 73728 | tf_op jit(solution)/shard_map/all_gather | solution.py:110
  217.6 0.9 fusion.15
  219.8 33.1 %all-reduce.13.cloned.1.call-done = f32[16384]{0:T(1024)} async-done(((f32[16384]{0:T(1024)}), f32[16384]{0:T(1024)}) %all-reduce.13.cloned.1.call-update) | async-done | bytes 65552 | tf_op jit(solution)/shard_map/psum | solution.py:82
  252.9 1.3 multiply_reduce_fusion
  254.3 1.0 convolution_bitcast_fusion.4
  255.3 40.3 %all-reduce.1 = (f32[65]{0:T(128)S(1)}, f32[]{:T(128)}) all-reduce(f32[65]{0:T(128)S(1)} %convolution_bitcast_fusion.4, f32[]{:T(128)} %get-tuple-element.19), channel_id=1, replica_groups=mesh['row'=8,'col'=4] {'row','col'}, use_global_device_ids=true, to_apply=%region_11.12 | all-reduce | flops 66 | bytes 528 | tf_op jit(solution)/shard_map/psum | solution.py:12
  297.1 0.9 fusion.11
  300.1 13.3 %all_gather.11 = f32[16384]{0:T(1024)S(1)} all-gather(f32[4096]{0:T(1024)S(1)} %subtract_divide_fusion), channel_id=1, replica_groups=mesh['row'=8,'col'=4] {'col'}, dimensions={0}, use_global_device_ids=true | all-gather | bytes 81920 | tf_op jit(solution)/shard_map/all_gather | solution.py:89
  315.8 53.1 %all-reduce.15.cloned.1.call-done = f32[16384]{0:T(1024)} async-done(((f32[16384]{0:T(1024)}), f32[16384]{0:T(1024)}) %all-reduce.15.cloned.1.call-update) | async-done | bytes 65552 | tf_op jit(solution)/shard_map/psum | solution.py:102
  368.9 1.3 multiply_reduce_fusion.2
  370.8 39.5 %all-reduce = (f32[66]{0:T(128)S(1)}, f32[]{:T(128)}) all-reduce(f32[66]{0:T(128)S(1)} %convolution_bitcast_fusion.14, f32[]{:T(128)} %get-tuple-element.17), channel_id=1, replica_groups=mesh['row'=8,'col'=4] {'row','col'}, use_global_device_ids=true, to_apply=%region_15.16 | all-reduce | flops 67 | bytes 536 | tf_op jit(solution)/shard_map/psum | solution.py:12
  411.5 0.9 fusion.12
  (60 shorter events, 16.6 us)
Async XLA Ops:
  7.2 1.8 copy-start
  7.2 40.9 %all-reduce.9.cloned.1.call-start = ((), (), s32[]{:S(2)}) async-start(), calls=%async_computation | async-start | bytes 131072 | tf_op jit(solution)/shard_map/psum | solution.py:82
  10.9 151.3 %all-reduce.11.cloned.1.call-start = ((), (), s32[]{:S(2)}) async-start(), calls=%async_computation.1 | async-start | bytes 131072 | tf_op jit(solution)/shard_map/psum | solution.py:102
  11.0 3.6 copy-start.2
  13.8 35.6 %copy-start.1 = (f32[64,4096]{1,0:T(8,128)S(1)}, f32[64,4096]{1,0:T(8,128)}, u32[]{:S(2)}) copy-start(f32[64,4096]{1,0:T(8,128)} %param.7) | copy-start | bytes 3145732
  109.4 143.5 %all-reduce.13.cloned.1.call-start = ((), (), s32[]{:S(2)}) async-start(), calls=%async_computation.2 | async-start | bytes 131072 | tf_op jit(solution)/shard_map/psum | solution.py:82
  219.5 149.4 %all-reduce.15.cloned.1.call-start = ((), (), s32[]{:S(2)}) async-start(), calls=%async_computation.3 | async-start | bytes 131072 | tf_op jit(solution)/shard_map/psum | solution.py:102
Sparse Core Ops, SparseCore 0:
  11.0 37.0 all-reduce.8
  109.5 52.6 all-reduce.10
  219.6 33.2 all-reduce.12
  315.9 52.9 all-reduce.14
where the time goes:
time: 424 us; the launch traced here: 422 us
  blocking collectives  197 us (46%)
  waiting for transfers between devices  171 us (40%)
  between operations  22.1 us (5%)
  matrix products  19.7 us (5%)
  other arithmetic  7.56 us (2%)
  local copies, waits for them, and re-layouts  4.67 us (1%)
    psum x4, blocking collectives, project_gram(): lax.psum((jnp.dot(basis, share, precision=HIGHEST), jnp.sum(share * share...  160 us
    psum x2, waiting for transfers between devices, shards(): whole = lax.psum(backward_now, 'row')  106 us
    psum x2, waiting for transfers between devices, shards(): left_whole = lax.psum(forward_now, 'col')  65.8 us
    all_gather x2, blocking collectives, shards(): join_joined = lax.all_gather(left_unit, 'col', axis=0, tiled=True)  26.6 us
    all_gather x1, blocking collectives, shards(): joined = lax.all_gather(right_unit, 'row', axis=0, tiled=True)  9.99 us
  transfers between devices with their start and end apart: 4, of which 4 were waited for; matrix products, arithmetic and copies ran while one was open for 1% of the time, Pallas kernels for 0%

commit v1 on v0

--- a/solution.py
+++ b/solution.py
@@ -10,7 +10,7 @@
 
 def project_gram(share, basis, gram, total):
     coeffs, squares = lax.psum(
-        (jnp.dot(basis, share, precision=HIGHEST), jnp.sum(share * share)), ("row", "col")
+        lax.psum((jnp.dot(basis, share, precision=HIGHEST), jnp.sum(share * share)), "col"), "row"
     )
     coeffs = coeffs / total
     squares = squares / total

time: 424 us -> 363 us (0.86)
  waiting for transfers between devices: 171 us -> 133 us
  blocking collectives: 197 us -> 175 us
    psum x4, blocking collectives: 160 us -> 46.8 us  [project_gram(): lax.psum((jnp.dot(basis, share, precision=HIGHEST), jnp.sum(share * share...]
    psum x0 -> x5, blocking collectives: none -> 92.9 us  [the longest x4 49.7 us: project_gram(): lax.psum(lax.psum((jnp.dot(basis, share, precision=HIGHEST), jnp.sum(shar...]
    psum x2, waiting for transfers between devices: 65.8 us -> 31.4 us  [shards(): left_whole = lax.psum(forward_now, 'col')]
  transfers between devices with their start and end apart: 4 -> 4, of which waited for: 4 -> 3; matrix products, arithmetic and copies ran while one was open for 1% -> 1% of each run, Pallas kernels for 0% -> 0%
where the time goes in v1:
time: 363 us; the launch traced here: 362 us
  blocking collectives  175 us (48%)
  waiting for transfers between devices  133 us (37%)
  between operations  22.1 us (6%)
  matrix products  19.7 us (5%)
  other arithmetic  7.57 us (2%)
  local copies, waits for them, and re-layouts  4.66 us (1%)
    psum x2, waiting for transfers between devices, shards(): whole = lax.psum(backward_now, 'row')  102 us
    psum x4, blocking collectives, project_gram(): lax.psum(lax.psum((jnp.dot(basis, share, precision=HIGHEST), jnp.sum(shar...  49.7 us
    psum x4, blocking collectives, project_gram(): lax.psum((jnp.dot(basis, share, precision=HIGHEST), jnp.sum(share * share...  46.8 us
    psum x1, blocking collectives, shards(): lax.psum((jnp.dot(left_basis, left_basis.T, precision=HIGHEST), jnp.dot(r...  43.2 us
    psum x2, waiting for transfers between devices, shards(): left_whole = lax.psum(forward_now, 'col')  31.4 us
    all_gather x2, blocking collectives, shards(): join_joined = lax.all_gather(left_unit, 'col', axis=0, tiled=True)  26.4 us
    all_gather x1, blocking collectives, shards(): joined = lax.all_gather(right_unit, 'row', axis=0, tiled=True)  8.62 us
  transfers between devices with their start and end apart: 4, of which 3 were waited for; matrix products, arithmetic and copies ran while one was open for 1% of the time, Pallas kernels for 0%

profile of v1, /device:TPU:0, one launch (start us, length us, event | category | flops | bytes accessed | tf_op | source)
XLA Modules:
  0.0 362.0 jit_solution(5567283080896087401)
XLA Ops:
  7.9 1.0 fusion.30
  9.0 0.9 fusion.19
  11.0 2.8 fusion.72
  15.4 43.2 %all-reduce = (f32[64,64]{1,0:T(8,128)S(1)}, f32[65,65]{1,0:T(8,128)S(1)}) all-reduce(f32[64,64]{1,0:T(8,128)S(1)} %fusion.72, f32[65,65]{1,0:T(8,128)S(1)} %fusion.23), channel_id=1, replica_groups=mesh['row'=8,'col'=4] {'row','col'}, use_global_device_ids=true, to_apply=%region_3.4 | all-reduce | flops 8321 | bytes 66568 | tf_op jit(solution)/shard_map/psum | solution.py:70
  58.6 1.3 multiply_reduce_fusion.1
  60.9 11.1 %all-reduce.8 = (f32[64]{0:T(128)S(1)}, f32[]{:T(128)}) all-reduce(f32[64]{0:T(128)S(1)} %convolution_bitcast_fusion.5, f32[]{:T(128)} %get-tuple-element.31), channel_id=1, replica_groups=mesh['row'=8,'col'=4] {'col'}, use_global_device_ids=true, to_apply=%region_1.2 | all-reduce | flops 65 | bytes 520 | tf_op jit(solution)/shard_map/psum | solution.py:13
  72.0 12.4 %all-reduce.4 = (f32[64]{0:T(128)S(1)}, f32[]{:T(128)}) all-reduce(f32[64]{0:T(128)S(1)} %get-tuple-element.23, f32[]{:T(128)} %get-tuple-element.24), channel_id=1, replica_groups=mesh['row'=8,'col'=4] {'row'}, use_global_device_ids=true, to_apply=%region_2.3 | all-reduce | flops 65 | bytes 520 | tf_op jit(solution)/shard_map/psum | solution.py:12
  88.0 13.2 %all_gather.9 = f32[16384]{0:T(1024)S(1)} all-gather(f32[4096]{0:T(1024)S(1)} %subtract_divide_fusion.1), channel_id=1, replica_groups=mesh['row'=8,'col'=4] {'col'}, dimensions={0}, use_global_device_ids=true | all-gather | bytes 81920 | tf_op jit(solution)/shard_map/all_gather | solution.py:89
  103.2 51.1 %all-reduce.16.cloned.1.call-done = f32[16384]{0:T(1024)} async-done(((f32[16384]{0:T(1024)}), f32[16384]{0:T(1024)}) %all-reduce.16.cloned.1.call-update) | async-done | bytes 65552 | tf_op jit(solution)/shard_map/psum | solution.py:102
  154.3 1.3 multiply_reduce_fusion.3
  156.2 12.3 %all-reduce.7 = (f32[65]{0:T(128)S(1)}, f32[]{:T(128)}) all-reduce(f32[65]{0:T(128)S(1)} %convolution_bitcast_fusion.15, f32[]{:T(128)} %get-tuple-element.29), channel_id=1, replica_groups=mesh['row'=8,'col'=4] {'col'}, use_global_device_ids=true, to_apply=%region_8.9 | all-reduce | flops 66 | bytes 528 | tf_op jit(solution)/shard_map/psum | solution.py:13
  168.5 12.4 %all-reduce.3 = (f32[65]{0:T(128)S(1)}, f32[]{:T(128)}) all-reduce(f32[65]{0:T(128)S(1)} %get-tuple-element.21, f32[]{:T(128)} %get-tuple-element.22), channel_id=1, replica_groups=mesh['row'=8,'col'=4] {'row'}, use_global_device_ids=true, to_apply=%region_9.10 | all-reduce | flops 66 | bytes 528 | tf_op jit(solution)/shard_map/psum | solution.py:12
  184.4 8.6 %all_gather.10 = f32[16384]{0:T(1024)S(1)} all-gather(f32[2048]{0:T(1024)S(1)} %subtract_divide_fusion.3), channel_id=1, replica_groups=mesh['row'=8,'col'=4] {'row'}, dimensions={0}, use_global_device_ids=true | all-gather | bytes 73728 | tf_op jit(solution)/shard_map/all_gather | solution.py:110
  193.2 0.9 fusion.15
  195.4 31.4 %all-reduce.18.cloned.1.call-done = f32[16384]{0:T(1024)} async-done(((f32[16384]{0:T(1024)}), f32[16384]{0:T(1024)}) %all-reduce.18.cloned.1.call-update) | async-done | bytes 65552 | tf_op jit(solution)/shard_map/psum | solution.py:82
  226.8 1.3 multiply_reduce_fusion
  228.1 1.0 convolution_bitcast_fusion.4
  229.2 11.1 %all-reduce.6 = (f32[65]{0:T(128)S(1)}, f32[]{:T(128)}) all-reduce(f32[65]{0:T(128)S(1)} %convolution_bitcast_fusion.4, f32[]{:T(128)} %get-tuple-element.27), channel_id=1, replica_groups=mesh['row'=8,'col'=4] {'col'}, use_global_device_ids=true, to_apply=%region_15.16 | all-reduce | flops 66 | bytes 528 | tf_op jit(solution)/shard_map/psum | solution.py:13
  240.3 12.4 %all-reduce.2 = (f32[65]{0:T(128)S(1)}, f32[]{:T(128)}) all-reduce(f32[65]{0:T(128)S(1)} %get-tuple-element.19, f32[]{:T(128)} %get-tuple-element.20), channel_id=1, replica_groups=mesh['row'=8,'col'=4] {'row'}, use_global_device_ids=true, to_apply=%region_16.17 | all-reduce | flops 66 | bytes 528 | tf_op jit(solution)/shard_map/psum | solution.py:12
  257.2 13.2 %all_gather.11 = f32[16384]{0:T(1024)S(1)} all-gather(f32[4096]{0:T(1024)S(1)} %subtract_divide_fusion), channel_id=1, replica_groups=mesh['row'=8,'col'=4] {'col'}, dimensions={0}, use_global_device_ids=true | all-gather | bytes 81920 | tf_op jit(solution)/shard_map/all_gather | solution.py:89
  272.8 50.5 %all-reduce.20.cloned.1.call-done = f32[16384]{0:T(1024)} async-done(((f32[16384]{0:T(1024)}), f32[16384]{0:T(1024)}) %all-reduce.20.cloned.1.call-update) | async-done | bytes 65552 | tf_op jit(solution)/shard_map/psum | solution.py:102
  323.4 1.3 multiply_reduce_fusion.2
  325.2 12.3 %all-reduce.5 = (f32[66]{0:T(128)S(1)}, f32[]{:T(128)}) all-reduce(f32[66]{0:T(128)S(1)} %convolution_bitcast_fusion.14, f32[]{:T(128)} %get-tuple-element.25), channel_id=1, replica_groups=mesh['row'=8,'col'=4] {'col'}, use_global_device_ids=true, to_apply=%region_21.22 | all-reduce | flops 67 | bytes 536 | tf_op jit(solution)/shard_map/psum | solution.py:13
  337.5 12.4 %all-reduce.1 = (f32[66]{0:T(128)S(1)}, f32[]{:T(128)}) all-reduce(f32[66]{0:T(128)S(1)} %get-tuple-element.17, f32[]{:T(128)} %get-tuple-element.18), channel_id=1, replica_groups=mesh['row'=8,'col'=4] {'row'}, use_global_device_ids=true, to_apply=%region_22.23 | all-reduce | flops 67 | bytes 536 | tf_op jit(solution)/shard_map/psum | solution.py:12
  (65 shorter events, 20.2 us)
Async XLA Ops:
  7.2 1.8 copy-start
  7.2 51.4 %all-reduce.14.cloned.1.call-start = ((), (), s32[]{:S(2)}) async-start(), calls=%async_computation | async-start | bytes 131072 | tf_op jit(solution)/shard_map/psum | solution.py:82
  10.9 143.4 %all-reduce.16.cloned.1.call-start = ((), (), s32[]{:S(2)}) async-start(), calls=%async_computation.1 | async-start | bytes 131072 | tf_op jit(solution)/shard_map/psum | solution.py:102
  11.0 3.6 %copy-start.2 = (f32[64,1,2048]{2,1,0:T(1,128)S(1)}, f32[64,1,2048]{2,1,0:T(1,128)}, u32[]{:S(2)}) copy-start(f32[64,1,2048]{2,1,0:T(1,128)} %param.8) | copy-start | bytes 1572868
  13.8 46.2 %copy-start.1 = (f32[64,4096]{1,0:T(8,128)S(1)}, f32[64,4096]{1,0:T(8,128)}, u32[]{:S(2)}) copy-start(f32[64,4096]{1,0:T(8,128)} %param.7) | copy-start | bytes 3145732
  102.9 123.9 %all-reduce.18.cloned.1.call-start = ((), (), s32[]{:S(2)}) async-start(), calls=%async_computation.2 | async-start | bytes 131072 | tf_op jit(solution)/shard_map/psum | solution.py:82
  195.1 128.2 %all-reduce.20.cloned.1.call-start = ((), (), s32[]{:S(2)}) async-start(), calls=%async_computation.3 | async-start | bytes 131072 | tf_op jit(solution)/shard_map/psum | solution.py:102
Sparse Core Ops, SparseCore 0:
  11.0 37.0 all-reduce.13
  103.0 51.2 all-reduce.15
  195.3 31.5 all-reduce.17
  272.9 50.4 all-reduce.19
